TPU v7x, 32 devices: a whole 2x2x4 slice. The times are simulated.
32 devices in a mesh: ri: 8 (over z, core), rj: 4 (over y, x).
Axes of the slice: x: 2, y: 2, z: 4, core: 2. Of those that a mesh axis runs over, the one named last changes fastest.
Arguments:
- pair: bfloat16 [320, 320, 128], P('ri', 'rj'), may hold values from -6 to 6
- in_gain: float32 [128], replicated, may hold values from 0.1 to 1.9
- in_bias: float32 [128], replicated, may hold values from -3 to 3
- w_in: bfloat16 [128, 512], replicated, may hold values from -0.5 to 0.5
- w_gate: bfloat16 [128, 128], replicated, may hold values from -0.5 to 0.5
- out_gain: float32 [128], replicated, may hold values from 0.1 to 1.9
- out_bias: float32 [128], replicated, may hold values from -3 to 3
- w_out: bfloat16 [128, 128], replicated, may hold values from -0.5 to 0.5
Outputs:
- update: bfloat16 [320, 320, 128], P('ri', 'rj')
All inputs are finite; a program needn't handle non-finite values.
Results may differ from a plain program's by a relative error of at most 0.015.
Values may be sent and summed in bfloat16 or wider, within the bound.
A program may use at most 128 MiB of HBM per device.

v0:
```python
import jax
import jax.numpy as jnp
from jax import lax
from jax.sharding import PartitionSpec as P


def layer_norm(values, gain, bias):
    mean = jnp.mean(values, axis=-1, keepdims=True)
    centered = values - mean
    var = jnp.mean(centered * centered, axis=-1, keepdims=True)
    return centered * lax.rsqrt(var + 1e-05) * gain + bias


def local(pair, in_gain, in_bias, w_in, w_gate, out_gain, out_bias, w_out):
    rows, cols, chans = pair.shape
    hidden = w_out.shape[0]
    normed = layer_norm(pair.astype(jnp.float32), in_gain, in_bias).astype(jnp.bfloat16)
    flat = normed.reshape(rows * cols, chans)
    proj = jnp.dot(flat, w_in, preferred_element_type=jnp.float32)
    a_tile = (
        (jax.nn.sigmoid(proj[:, hidden : 2 * hidden]) * proj[:, :hidden])
        .astype(jnp.bfloat16)
        .reshape(rows, cols, hidden)
    )
    b_tile = (
        (jax.nn.sigmoid(proj[:, 3 * hidden :]) * proj[:, 2 * hidden : 3 * hidden])
        .astype(jnp.bfloat16)
        .reshape(rows, cols, hidden)
    )
    gate = jax.nn.sigmoid(jnp.dot(flat, w_gate, preferred_element_type=jnp.float32)).astype(
        jnp.bfloat16
    )
    a_rows = lax.all_gather(a_tile, "rj", axis=1, tiled=True)
    product = lax.dot_general(
        a_rows, b_tile, (((0,), (0,)), ((2,), (2,))), preferred_element_type=jnp.float32
    )
    summed = lax.psum_scatter(
        jnp.transpose(product, (1, 2, 0)).astype(jnp.bfloat16),
        "ri",
        scatter_dimension=0,
        tiled=True,
    ).astype(jnp.float32)
    tri = summed.reshape(rows * cols, hidden)
    tri_normed = layer_norm(tri, out_gain, out_bias).astype(jnp.bfloat16)
    mixed = jnp.dot(tri_normed, w_out, preferred_element_type=jnp.float32)
    update = gate.astype(jnp.float32) * mixed
    return update.reshape(rows, cols, chans).astype(jnp.bfloat16)


def solution(mesh):
    return jax.shard_map(
        local,
        mesh=mesh,
        in_specs=(P("ri", "rj", None), P(), P(), P(), P(), P(), P(), P()),
        out_specs=P("ri", "rj", None),
        check_vma=False,
    )
```

profile of v0, /device:TPU:0, one launch (start us, length us, event | category | flops | bytes accessed | tf_op | source)
XLA Modules:
  0.0 174.6 jit_solution(12855295967835624654)
XLA Ops:
  6.5 0.0 copy-start
  6.5 0.0 copy-start.1
  6.5 0.0 copy-start.4
  6.5 0.0 copy-start.5
  6.5 0.0 all-gather.2.cloned.1.call-start
  6.6 1.6 convert_reduce_fusion
  8.2 2.3 %fusion.8 = f32[40,80]{1,0:T(8,128)S(1)} fusion(bf16[40,80,128]{2,1,0:T(8,128)(2,1)} %param.8, f32[40,80]{1,0:T(8,128)S(1)} %broadcast_multiply_fusion.1), kind=kLoop, calls=%fused_computation.13 | loop fusion | flops 1635200 | bytes 844800 | tf_op jit(solution)/shard_map/reduce_sum | solution.py:10
  10.6 0.0 copy-done.1
  10.6 0.0 copy-done.4
  10.6 0.0 copy-done.5
  10.6 1.1 fusion.11
  11.7 0.0 copy-done
  11.7 1.0 fusion.24
  12.7 0.9 fusion.12
  13.6 1.1 copy.28
  14.7 0.0 all-gather.2.cloned.1.call-update
  14.7 0.0 reduce-scatter.2.cloned.1.call-start
  14.8 1.6 copy.30
  16.4 46.1 %all-gather.2.cloned.1.call-done = bf16[40,320,128]{2,0,1:T(8,128)(2,1)} async-done(((bf16[40,80,128]{2,0,1:T(8,128)(2,1)}), bf16[40,320,128]{2,0,1:T(8,128)(2,1)}) %all-gather.2.cloned.1.call-update) | async-done | bytes 3276816 | tf_op jit(solution)/shard_map/all_gather | solution.py:33
  62.5 6.7 %copy.29 = bf16[40,320,128]{1,0,2:T(8,128)(2,1)} copy(bf16[40,320,128]{2,0,1:T(8,128)(2,1)} %all-gather.2.cloned.1.call-done) | data formatting | bytes 6553600 | tf_op jit(solution)/shard_map/all_gather | solution.py:33
  69.3 7.4 %convert_bitcast_fusion = bf16[320,80,128]{0,1,2:T(8,128)(2,1)} fusion(bf16[40,320,128]{1,0,2:T(8,128)(2,1)} %copy.29, bf16[40,80,128]{1,0,2:T(8,128)(2,1)S(1)} %copy.30), kind=kOutput, calls=%fused_computation | convolution fusion | flops 265420800 | bytes 10649600 | tf_op jit(solution)/shard_map/dot_general | solution.py:34
  76.7 11.5 %copy.31 = bf16[320,80,128]{2,1,0:T(8,128)(2,1)} copy(bf16[320,80,128]{0,1,2:T(8,128)(2,1)} %convert_bitcast_fusion) | data formatting | bytes 13107200 | tf_op jit(solution)/shard_map/convert_element_type | solution.py:38
  88.2 0.0 copy-start.8
  88.2 0.0 reduce-scatter.2.cloned.1.call-update
  88.2 0.7 copy-done.8
  89.0 0.6 fusion.4
  89.5 0.0 copy-start.6
  89.6 0.0 copy-start.7
  89.6 0.0 copy-start.3
  89.6 71.0 %reduce-scatter.2.cloned.1.call-done = bf16[40,80,128]{2,1,0:T(8,128)(2,1)} async-done(((bf16[320,80,128]{2,1,0:T(8,128)(2,1)}), bf16[40,80,128]{2,1,0:T(8,128)(2,1)}) %reduce-scatter.2.cloned.1.call-update) | async-done | bytes 819216 | tf_op jit(solution)/shard_map/reduce_scatter | solution.py:37
  160.6 0.0 copy-start.2
  160.6 1.6 convert_reduce_fusion.1
  162.2 0.1 div.29
  162.3 2.3 %multiply_reduce_fusion = f32[40,80]{1,0:T(8,128)S(1)} fusion(f32[40,80]{1,0:T(8,128)S(1)} %broadcast_multiply_fusion, bf16[40,80,128]{2,1,0:T(8,128)(2,1)} %reduce-scatter.2.cloned.1.call-done), kind=kLoop, calls=%fused_computation.34 | loop fusion | flops 1635200 | bytes 844800 | tf_op jit(solution)/shard_map/reduce_sum | solution.py:10
  164.7 0.1 rsqrt.21
  164.8 0.0 copy-done.6
  164.8 0.0 copy-done.7
  164.8 0.0 copy-done.2
  164.8 1.7 %fusion.23 = bf16[3200,128]{1,0:T(8,128)(2,1)S(1)} fusion(f32[128]{0:T(128)S(1)} %copy-done.6, f32[128]{0:T(128)S(1)} %copy-done.7, f32[3200]{0:T(1024)S(1)} %rsqrt.21, f32[3200]{0:T(1024)S(1)} %div.29, bf16[40,80,128]{2,1,0:T(8,128)(2,1)S(1)} %copy-done.2), kind=kLoop, calls=%fused_computation.33 | loop fusion | flops 2457600 | bytes 1665024 | tf_op jit(solution)/shard_map/convert_element_type | solution.py:44
  166.5 0.0 copy-done.3
  166.5 1.2 fusion.5
  (4 shorter events, 0.0 us)
Async XLA Ops:
  6.5 5.2 %copy-start = (bf16[128,512]{1,0:T(8,128)(2,1)S(1)}, bf16[128,512]{1,0:T(8,128)(2,1)}, u32[]{:S(2)}) copy-start(bf16[128,512]{1,0:T(8,128)(2,1)} %param.11) | copy-start | bytes 393220
  6.5 4.1 %copy-start.1 = (bf16[40,80,128]{2,1,0:T(8,128)(2,1)S(1)}, bf16[40,80,128]{2,1,0:T(8,128)(2,1)}, u32[]{:S(2)}) copy-start(bf16[40,80,128]{2,1,0:T(8,128)(2,1)} %param.8) | copy-start | bytes 2457604
  6.5 4.1 %copy-start.4 = (f32[128]{0:T(128)S(1)}, f32[128]{0:T(128)}, u32[]{:S(2)}) copy-start(f32[128]{0:T(128)} %param.10) | copy-start | bytes 1540
  6.5 4.1 %copy-start.5 = (f32[128]{0:T(128)S(1)}, f32[128]{0:T(128)}, u32[]{:S(2)}) copy-start(f32[128]{0:T(128)} %param.9) | copy-start | bytes 1540
  6.5 56.0 %all-gather.2.cloned.1.call-start = ((), (), s32[]{:S(2)}) async-start(), calls=%async_computation.1 | async-start | bytes 4096000 | tf_op jit(solution)/shard_map/all_gather | solution.py:33
  14.7 145.9 %reduce-scatter.2.cloned.1.call-start = ((), (), s32[]{:S(2)}) async-start(), calls=%async_computation.2 | async-start | bytes 7372800 | tf_op jit(solution)/shard_map/reduce_scatter | solution.py:37
  88.2 0.8 copy-start.8
  89.5 75.2 %copy-start.6 = (f32[128]{0:T(128)S(1)}, f32[128]{0:T(128)}, u32[]{:S(2)}) copy-start(f32[128]{0:T(128)} %param.14) | copy-start | bytes 1540
  89.6 75.2 %copy-start.7 = (f32[128]{0:T(128)S(1)}, f32[128]{0:T(128)}, u32[]{:S(2)}) copy-start(f32[128]{0:T(128)} %param.13) | copy-start | bytes 1540
  89.6 77.0 %copy-start.3 = (bf16[128,128]{1,0:T(8,128)(2,1)S(1)}, bf16[128,128]{1,0:T(8,128)(2,1)}, u32[]{:S(2)}) copy-start(bf16[128,128]{1,0:T(8,128)(2,1)} %param.15) | copy-start | bytes 98308
  160.6 4.2 %copy-start.2 = (bf16[40,80,128]{2,1,0:T(8,128)(2,1)S(1)}, bf16[40,80,128]{2,1,0:T(8,128)(2,1)}, u32[]{:S(2)}) copy-start(bf16[40,80,128]{2,1,0:T(8,128)(2,1)} %reduce-scatter.2.cloned.1.call-done) | copy-start | bytes 2457604
Sparse Core Ops, SparseCore 0:
  14.8 47.6 all-gather.1
  88.4 72.1 reduce-scatter.1
where the time goes:
time: 175 us
  waiting for transfers between devices  117 us (67%)
  local copies, waits for them, and re-layouts  21.9 us (13%)
  between operations  13.6 us (8%)
  other arithmetic  11.7 us (7%)
  matrix products  10.2 us (6%)
    reduce_scatter x1, waiting for transfers between devices, local(): lax.psum_scatter(jnp.transpose(product, (1, 2, 0)).astype(jnp.bfloat16),...  71 us
    all_gather x1, waiting for transfers between devices, local(): a_rows = lax.all_gather(a_tile, 'rj', axis=1, tiled=True)  46.1 us
    convert_element_type x1, local copies, waits for them, and re-layouts, local(): jnp.transpose(product, (1, 2, 0)).astype(jnp.bfloat16)  11.5 us
    dot_general x1, matrix products, local(): lax.dot_general(a_rows, b_tile, (((0,), (0,)), ((2,), (2,))), preferred_e...  7.43 us
    all_gather x1, local copies, waits for them, and re-layouts, local(): a_rows = lax.all_gather(a_tile, 'rj', axis=1, tiled=True)  6.75 us
    reduce_sum x2, other arithmetic, layer_norm(): var = jnp.mean(centered * centered, axis=-1, keepdims=True)  4.67 us
  transfers between devices with their start and end apart: 2, of which 2 were waited for; matrix products, arithmetic and copies ran while one was open for 1% of the time, Pallas kernels for 0%

commit v1 on v0

--- a/solution.py
+++ b/solution.py
@@ -2,6 +2,24 @@
 import jax.numpy as jnp
 from jax import lax
 from jax.sharding import PartitionSpec as P
+
+
+def in_order(blocks, dim):
+    lengths = list(blocks.shape[1:])
+    lengths[dim] *= blocks.shape[0]
+    return jnp.moveaxis(blocks, 0, dim).reshape(lengths)
+
+
+def grow_blocks(shard, axis):
+    count = lax.axis_size(axis)
+    tiles = shard[None]
+    for level in range(count.bit_length() - 1):
+        distance = 1 << level
+        received = lax.ppermute(tiles, axis, [(i, i ^ distance) for i in range(count)])
+        both = jnp.stack([tiles, received])
+        upper = lax.axis_index(axis) >> level & 1
+        tiles = jnp.where(upper == 0, both, both[::-1]).reshape(-1, *shard.shape)
+    return tiles
 
 
 def layer_norm(values, gain, bias):
@@ -30,7 +48,7 @@
     gate = jax.nn.sigmoid(jnp.dot(flat, w_gate, preferred_element_type=jnp.float32)).astype(
         jnp.bfloat16
     )
-    a_rows = lax.all_gather(a_tile, "rj", axis=1, tiled=True)
+    a_rows = in_order(grow_blocks(a_tile, "rj"), 1)
     product = lax.dot_general(
         a_rows, b_tile, (((0,), (0,)), ((2,), (2,))), preferred_element_type=jnp.float32
     )

time: 175 us -> 190 us (1.086)
  waiting for transfers between devices: 117 us -> 123 us
  starting transfers between devices: 0.08 us -> 4.83 us
  other arithmetic: 11.7 us -> 15.8 us
    ppermute x0 -> x2, waiting for transfers between devices: none -> 51.6 us  [grow_blocks(): lax.ppermute(tiles, axis, [(i, i ^ distance) for i in range(count)])]
    all_gather x1 -> x0, waiting for transfers between devices: 46.1 us -> none  [local(): a_rows = lax.all_gather(a_tile, 'rj', axis=1, tiled=True)]
    all_gather x1 -> x0, local copies, waits for them, and re-layouts: 6.75 us -> none  [local(): a_rows = lax.all_gather(a_tile, 'rj', axis=1, tiled=True)]
    ppermute x0 -> x2, starting transfers between devices: none -> 4.8 us  [grow_blocks(): lax.ppermute(tiles, axis, [(i, i ^ distance) for i in range(count)])]
    another operation x0 -> x3, other arithmetic: none -> 3.48 us  [grow_blocks(): both = jnp.stack([tiles, received])]
    reshape x1, local copies, waits for them, and re-layouts: 1.1 us -> 4.28 us  [in_order(): return jnp.moveaxis(blocks, 0, dim).reshape(lengths)]
  transfers between devices with their start and end apart: 2 -> 3, of which waited for: 2 -> 3; matrix products, arithmetic and copies ran while one was open for 1% -> 1% of each run, Pallas kernels for 0% -> 0%
where the time goes in v1:
time: 190 us; the launch traced here: 189 us
  waiting for transfers between devices  123 us (65%)
  local copies, waits for them, and re-layouts  21 us (11%)
  other arithmetic  15.8 us (8%)
  between operations  13.6 us (7%)
  matrix products  10.6 us (6%)
  starting transfers between devices  4.83 us (3%)
    reduce_scatter x1, waiting for transfers between devices, local(): lax.psum_scatter(jnp.transpose(product, (1, 2, 0)).astype(jnp.bfloat16),...  71.8 us
    ppermute x2, waiting for transfers between devices, grow_blocks(): lax.ppermute(tiles, axis, [(i, i ^ distance) for i in range(count)])  51.6 us
    convert_element_type x1, local copies, waits for them, and re-layouts, local(): jnp.transpose(product, (1, 2, 0)).astype(jnp.bfloat16)  11.4 us
    dot_general x1, matrix products, local(): lax.dot_general(a_rows, b_tile, (((0,), (0,)), ((2,), (2,))), preferred_e...  7.81 us
    ppermute x2, starting transfers between devices, grow_blocks(): lax.ppermute(tiles, axis, [(i, i ^ distance) for i in range(count)])  4.8 us
    reduce_sum x2, other arithmetic, layer_norm(): var = jnp.mean(centered * centered, axis=-1, keepdims=True)  4.67 us
    reshape x1, local copies, waits for them, and re-layouts, in_order(): return jnp.moveaxis(blocks, 0, dim).reshape(lengths)  4.28 us
  transfers between devices with their start and end apart: 3, of which 3 were waited for; matrix products, arithmetic and copies ran while one was open for 1% of the time, Pallas kernels for 0%

profile of v1, /device:TPU:0, one launch (start us, length us, event | category | flops | bytes accessed | tf_op | source)
XLA Modules:
  0.0 189.3 jit_solution(15484176646308829196)
XLA Ops:
  6.5 0.0 copy-start
  6.5 0.0 copy-start.1
  6.5 0.0 copy-start.6
  6.5 0.0 copy-start.7
  6.5 0.0 reduce-scatter.2.cloned.1.call-start
  6.6 1.6 convert_reduce_fusion
  8.2 2.3 %fusion.8 = f32[40,80]{1,0:T(8,128)S(1)} fusion(bf16[40,80,128]{2,1,0:T(8,128)(2,1)} %param.8, f32[40,80]{1,0:T(8,128)S(1)} %broadcast_multiply_fusion.1), kind=kLoop, calls=%fused_computation.16 | loop fusion | flops 1635200 | bytes 844800 | tf_op jit(solution)/shard_map/reduce_sum | solution.py:28
  10.6 0.0 copy-done.1
  10.6 0.0 copy-done.6
  10.6 0.0 copy-done.7
  10.6 1.1 fusion.11
  11.7 0.0 copy-start.3
  11.7 0.9 copy-done.3
  12.6 0.0 copy-done
  12.6 1.0 fusion.26
  13.6 0.9 fusion.12
  14.5 3.0 %collective-permute-start = (bf16[1,40,80,128]{3,2,1,0:T(8,128)(2,1)S(1)}, bf16[1,40,80,128]{3,2,1,0:T(8,128)(2,1)S(1)}, u32[]{:S(2)}, u32[]{:S(2)}) collective-permute-start(bf16[1,40,80,128]{3,2,1,0:T(8,128)(2,1)S(1)} %bitcast.39), channel_id=1, source_target_pairs={{0,1},{1,0},{2,3},{3,2},{4,5},{5,4},{6,7},{7,6},{8,9},{9,8},{10,11... | collective-permute-start | bytes 2457608 | tf_op jit(solution)/shard_map/ppermute | solution.py:18
  17.5 18.2 %collective-permute-done = bf16[1,40,80,128]{3,2,1,0:T(8,128)(2,1)S(1)} collective-permute-done((bf16[1,40,80,128]{3,2,1,0:T(8,128)(2,1)S(1)}, bf16[1,40,80,128]{3,2,1,0:T(8,128)(2,1)S(1)}, u32[]{:S(2)}, u32[]{:S(2)}) %collective-permute-start) | collective-permute-done | bytes 819232 | tf_op jit(solution)/shard_map/ppermute | solution.py:18
  35.7 0.2 pad_maximum_fusion.1
  35.9 1.6 fusion.25
  37.5 1.8 collective-permute-start.1
  39.3 2.1 %copy.31 = bf16[40,80,128]{1,0,2:T(8,128)(2,1)} copy(bf16[40,80,128]{2,1,0:T(8,128)(2,1)S(1)} %bitcast.41) | data formatting | bytes 1638400 | tf_op jit(solution)/shard_map/reshape | solution.py:46
  41.4 33.4 %collective-permute-done.1 = bf16[2,40,80,128]{3,2,1,0:T(8,128)(2,1)} collective-permute-done((bf16[2,40,80,128]{3,2,1,0:T(8,128)(2,1)}, bf16[2,40,80,128]{3,2,1,0:T(8,128)(2,1)}, u32[]{:S(2)}, u32[]{:S(2)}) %collective-permute-start.1) | collective-permute-done | bytes 1638432 | tf_op jit(solution)/shard_map/ppermute | solution.py:18
  74.8 1.7 pad_maximum_fusion
  76.5 0.6 reverse_select_fusion
  77.2 1.0 copy.29
  78.1 4.3 %copy.30 = bf16[40,320,128]{1,0,2:T(8,128)(2,1)} copy(bf16[40,320,128]{2,1,0:T(8,128)(2,1)S(1)} %bitcast.36) | data formatting | bytes 6553600 | tf_op jit(solution)/shard_map/reshape | solution.py:10
  82.4 7.8 %convert_bitcast_fusion = bf16[320,80,128]{0,1,2:T(8,128)(2,1)} fusion(bf16[40,320,128]{1,0,2:T(8,128)(2,1)} %copy.30, bf16[40,80,128]{1,0,2:T(8,128)(2,1)} %copy.31), kind=kOutput, calls=%fused_computation | convolution fusion | flops 265420800 | bytes 10649600 | tf_op jit(solution)/shard_map/dot_general | solution.py:52
  90.2 11.4 %copy.32 = bf16[320,80,128]{2,1,0:T(8,128)(2,1)} copy(bf16[320,80,128]{0,1,2:T(8,128)(2,1)} %convert_bitcast_fusion) | data formatting | bytes 13107200 | tf_op jit(solution)/shard_map/convert_element_type | solution.py:56
  101.7 0.0 copy-start.4
  101.7 0.0 reduce-scatter.2.cloned.1.call-update
  101.7 1.1 copy-done.4
  102.8 0.0 copy-done.10
  102.8 0.6 fusion.4
  103.4 0.0 copy-start.8
  103.4 0.0 copy-start.9
  103.4 0.0 copy-start.5
  103.4 71.8 %reduce-scatter.2.cloned.1.call-done = bf16[40,80,128]{2,1,0:T(8,128)(2,1)} async-done(((bf16[320,80,128]{2,1,0:T(8,128)(2,1)}), bf16[40,80,128]{2,1,0:T(8,128)(2,1)}) %reduce-scatter.2.cloned.1.call-update) | async-done | bytes 819216 | tf_op jit(solution)/shard_map/reduce_scatter | solution.py:55
  175.3 1.6 convert_reduce_fusion.1
  176.9 0.1 div.29
  177.0 2.3 %multiply_reduce_fusion = f32[40,80]{1,0:T(8,128)S(1)} fusion(f32[40,80]{1,0:T(8,128)S(1)} %broadcast_multiply_fusion, bf16[40,80,128]{2,1,0:T(8,128)(2,1)} %reduce-scatter.2.cloned.1.call-done), kind=kLoop, calls=%fused_computation.38 | loop fusion | flops 1635200 | bytes 844800 | tf_op jit(solution)/shard_map/reduce_sum | solution.py:28
  179.4 0.1 rsqrt.21
  179.4 0.0 copy-done.8
  179.4 0.0 copy-done.9
  179.5 0.0 copy-done.2
  179.5 1.7 fusion.23
  181.2 0.0 copy-done.5
  181.2 1.3 fusion.5
  (6 shorter events, 0.0 us)
Async XLA Ops:
  6.5 6.1 %copy-start = (bf16[128,512]{1,0:T(8,128)(2,1)S(1)}, bf16[128,512]{1,0:T(8,128)(2,1)}, u32[]{:S(2)}) copy-start(bf16[128,512]{1,0:T(8,128)(2,1)} %param.11) | copy-start | bytes 393220
  6.5 4.1 %copy-start.1 = (bf16[40,80,128]{2,1,0:T(8,128)(2,1)S(1)}, bf16[40,80,128]{2,1,0:T(8,128)(2,1)}, u32[]{:S(2)}) copy-start(bf16[40,80,128]{2,1,0:T(8,128)(2,1)} %param.8) | copy-start | bytes 2457604
  6.5 4.1 %copy-start.6 = (f32[128]{0:T(128)S(1)}, f32[128]{0:T(128)}, u32[]{:S(2)}) copy-start(f32[128]{0:T(128)} %param.10) | copy-start | bytes 1540
  6.5 4.1 %copy-start.7 = (f32[128]{0:T(128)S(1)}, f32[128]{0:T(128)}, u32[]{:S(2)}) copy-start(f32[128]{0:T(128)} %param.9) | copy-start | bytes 1540
  6.5 168.7 %reduce-scatter.2.cloned.1.call-start = ((), (), s32[]{:S(2)}) async-start(), calls=%async_computation.1 | async-start | bytes 7372800 | tf_op jit(solution)/shard_map/reduce_scatter | solution.py:55
  11.7 0.9 copy-start.3
  14.5 21.3 %collective-permute-start = (bf16[1,40,80,128]{3,2,1,0:T(8,128)(2,1)S(1)}, bf16[1,40,80,128]{3,2,1,0:T(8,128)(2,1)S(1)}, u32[]{:S(2)}, u32[]{:S(2)}) collective-permute-start(bf16[1,40,80,128]{3,2,1,0:T(8,128)(2,1)S(1)} %bitcast.39), channel_id=1, source_target_pairs={{0,1},{1,0},{2,3},{3,2},{4,5},{5,4},{6,7},{7,6},{8,9},{9,8},{10,11... | collective-permute-start | bytes 2457608 | tf_op jit(solution)/shard_map/ppermute | solution.py:18
  37.5 37.3 %collective-permute-start.1 = (bf16[2,40,80,128]{3,2,1,0:T(8,128)(2,1)}, bf16[2,40,80,128]{3,2,1,0:T(8,128)(2,1)}, u32[]{:S(2)}, u32[]{:S(2)}) collective-permute-start(bf16[2,40,80,128]{3,2,1,0:T(8,128)(2,1)} %get-tuple-element.8), channel_id=1, source_target_pairs={{0,2},{1,3},{2,0},{3,1},{4,6},{5,7},{6,4},{7,5},{8,10},{9,11},{10,... | collective-permute-start | bytes 4915208 | tf_op jit(solution)/shard_map/ppermute | solution.py:18
  101.7 1.1 copy-start.4
  101.7 1.1 copy-start.10
  103.4 76.1 %copy-start.8 = (f32[128]{0:T(128)S(1)}, f32[128]{0:T(128)}, u32[]{:S(2)}) copy-start(f32[128]{0:T(128)} %param.14) | copy-start | bytes 1540
  103.4 76.0 %copy-start.9 = (f32[128]{0:T(128)S(1)}, f32[128]{0:T(128)}, u32[]{:S(2)}) copy-start(f32[128]{0:T(128)} %param.13) | copy-start | bytes 1540
  103.4 77.8 %copy-start.5 = (bf16[128,128]{1,0:T(8,128)(2,1)S(1)}, bf16[128,128]{1,0:T(8,128)(2,1)}, u32[]{:S(2)}) copy-start(bf16[128,128]{1,0:T(8,128)(2,1)} %param.15) | copy-start | bytes 98308
  175.3 4.2 %copy-start.2 = (bf16[40,80,128]{2,1,0:T(8,128)(2,1)S(1)}, bf16[40,80,128]{2,1,0:T(8,128)(2,1)}, u32[]{:S(2)}) copy-start(bf16[40,80,128]{2,1,0:T(8,128)(2,1)} %reduce-scatter.2.cloned.1.call-done) | copy-start | bytes 2457604
Sparse Core Ops, SparseCore 0:
  101.8 73.4 reduce-scatter.1
